TPU v7x, 32 devices: a whole 2x2x4 slice. The times are simulated.
32 devices in a mesh: region: 4 (over y, x), cluster: 8 (over z, core).
Axes of the slice: x: 2, y: 2, z: 4, core: 2. Of those that a mesh axis runs over, the one named last changes fastest.
Arguments:
- pilots: bfloat16 [128, 1024, 1024], P(('region', 'cluster')), may hold values from -0.1875 to 0.1875
- estimate: bfloat16 [128, 8, 1024], P(('region', 'cluster')), may hold values from -6 to 6
- visible: int32 [128, 1024], P(('region', 'cluster')), may hold values from 0 to 65535, as said below
- blocks: int32 [128], P(('region', 'cluster')), may hold values from 4 to 8
- received: float32 [128, 8, 1024], P(('region', 'cluster')), may hold values from -6 to 6
- previous: float32 [128, 8, 1024], P(('region', 'cluster')), may hold values from -6 to 6
- onsager: float32 [128], P(('region', 'cluster')), may hold values from 0.2 to 0.8
- user_cluster: int32 [65536], replicated, may hold values from 0 to 15
- cluster_prior: float32 [16], replicated, may hold values from -4 to 0
Outputs:
- new_estimate: bfloat16 [128, 8, 1024], P(('region', 'cluster'))
- residual: float32 [128, 8, 1024], P(('region', 'cluster'))
- posterior: float32 [65536], P(('region', 'cluster'))
Inputs may be any that keep to these rules, and one draw needn't show every extreme that they name: Every draw has some access point with 8 live blocks. `visible`: users are numbered region by region, 2048 * 8 to a region, in the order of the devices along region+cluster. An access point hears only users of its own region or of the two regions beside it along region (the first and the last region are beside each other); most of the users it hears are of its own region.
All inputs are finite; a program needn't handle non-finite values.
Results may differ from a plain program's by a relative error of at most 0.0056.
Values sent between devices are 32-bit elements; how exact they have to be, the bound alone decides.
A program may use at most 192 MiB of HBM per device.

v0:
```python
import jax
import jax.numpy as jnp
from jax import lax
from jax.sharding import PartitionSpec as P

ROW_BLOCK = 128
U_DEV = 2048
epsilon = 1e-06


def passed_along(block, axis, distance):
    devices = range(lax.axis_size(axis))
    route = [((i - distance) % len(devices), i) for i in devices]
    return lax.ppermute(block, axis, route)


def decide(summed, start, count, user_cluster, cluster_prior):
    labels = lax.dynamic_slice_in_dim(user_cluster, start, count)
    table = jnp.arange(cluster_prior.shape[0], dtype=jnp.int32)
    prior = jnp.sum(
        jnp.where(labels[:, None] == table[None, :], cluster_prior[None, :], jnp.float32(0.0)),
        axis=1,
    )
    return jax.nn.sigmoid(summed + prior)


def local(
    pilots, estimate, visible, blocks, received, previous, onsager, user_cluster, cluster_prior
):
    points, antennas, slots = estimate.shape
    live = jnp.arange(slots)[None, :] // ROW_BLOCK < blocks[:, None]
    masked = jnp.where(live[:, None, :], estimate, jnp.zeros_like(estimate))
    widened = masked.astype(jnp.float32)
    product = jnp.einsum("amr,arl->aml", masked, pilots, preferred_element_type=jnp.float32)
    resid = received - product + onsager[:, None, None] * previous
    spread = jnp.mean(resid * resid, axis=(1, 2)) + epsilon
    narrow = resid.astype(jnp.bfloat16)
    stat = widened + jnp.einsum("aml,arl->amr", narrow, pilots, preferred_element_type=jnp.float32)
    energy = jnp.sum(stat * stat, axis=1)
    base = 0.5 * antennas * jnp.log(spread / (1.0 + spread))
    llr = base[:, None] + energy / (2.0 * spread * (1.0 + spread))[:, None]
    llr = jnp.where(live, llr, jnp.float32(0.0))
    total_users = U_DEV * lax.axis_size("region") * lax.axis_size("cluster")
    own_start = lax.axis_index(("region", "cluster")) * U_DEV
    flat_llr = llr.reshape(-1)
    region_users = U_DEV * lax.axis_size("cluster")
    regions = lax.axis_size("region")
    lowest = (lax.axis_index("region") + regions - 1) % regions * region_users
    relative = (visible - lowest + total_users) % total_users
    window = jax.ops.segment_sum(flat_llr, relative.reshape(-1), num_segments=3 * region_users)
    from_below = passed_along(window[2 * region_users :], "region", 1)
    from_above = passed_along(window[:region_users], "region", -1)
    region_sum = window[region_users : 2 * region_users] + from_below + from_above
    owned_sum = lax.psum_scatter(region_sum, "cluster", scatter_dimension=0, tiled=True)
    owned = decide(owned_sum, own_start, U_DEV, user_cluster, cluster_prior)
    own_post = lax.all_gather(owned, "cluster", axis=0, tiled=True)
    below = passed_along(own_post, "region", 1)
    above = passed_along(own_post, "region", -1)
    nearby = jnp.concatenate([below, own_post, above])
    rate = nearby[relative]
    fresh = rate[:, None, :] * stat / (1.0 + spread)[:, None, None]
    new_estimate = jnp.where(live[:, None, :], fresh, jnp.float32(0.0)).astype(jnp.bfloat16)
    return (new_estimate, resid, owned)


def solution(mesh):
    placed = (
        P(("region", "cluster"), None, None),
        P(("region", "cluster"), None, None),
        P(("region", "cluster"), None),
        P(("region", "cluster")),
        P(("region", "cluster"), None, None),
        P(("region", "cluster"), None, None),
        P(("region", "cluster")),
        P(),
        P(),
    )
    return jax.shard_map(
        local,
        mesh=mesh,
        in_specs=placed,
        out_specs=(
            P(("region", "cluster"), None, None),
            P(("region", "cluster"), None, None),
            P(("region", "cluster")),
        ),
        check_vma=False,
    )
```

profile of v0, /device:TPU:0, one launch (start us, length us, event | category | flops | bytes accessed | tf_op | source)
XLA Modules:
  0.0 153.7 jit_solution(528623752502533669)
XLA Ops:
  7.2 0.0 all-reduce.3.cloned.1.call-start
  7.3 0.9 fusion.7
  8.2 0.9 broadcast_compare_fusion
  9.1 5.3 %multiply_reduce_fusion.1 = (f32[4]{0:T(128)S(1)}, f32[4,8,1024]{2,1,0:T(8,128)S(1)}) fusion(f32[4,8,1024]{2,1,0:T(8,128)} %param.14, f32[4]{0:T(128)} %param.15, f32[4,8,1024]{2,1,0:T(8,128)} %param.13, bf16[4,1024,1024]{2,1,0:T(8,128)(2,1)} %param.9, bf16[4,8,1024]{2,1,0:T(8,128)(2,1)} %param.10, pred[4,1024]{1,0:T(4,128)(4,1)S(1)} %broadcast_compare_fusion), kind=kOutput, calls=%fused_computation.10 | convolution fusion | flops 67305472 | bytes 8851488 | tf_op jit(solution)/shard_map/amr,arl->aml/dot_general | solution.py:34
  14.4 2.3 %multiply_reduce_fusion = (f32[4,1024]{1,0:T(4,128)S(1)}, f32[4,8,1024]{2,1,0:T(8,128)S(1)}) fusion(bf16[4,1024,1024]{2,1,0:T(8,128)(2,1)S(1)} %copy-done, f32[4,8,1024]{2,1,0:T(8,128)S(1)} %get-tuple-element.11, bf16[4,8,1024]{2,1,0:T(8,128)(2,1)S(1)} %copy-done.2, pred[4,1024]{1,0:T(4,128)(4,1)S(1)} %broadcast_compare_fusion), kind=kOutput, calls=%fused_computation.9 | convolution fusion | flops 67301376 | bytes 8736768 | tf_op jit(solution)/shard_map/aml,arl->amr/dot_general | solution.py:38
  16.7 0.1 select_bitcast_fusion
  16.8 21.9 %scatter_custom_fusion = f32[49152]{0:T(1024)S(1)} fusion(s32[4096]{0:T(1024)S(1)} %bitcast.17, f32[4096]{0:T(1024)S(1)} %bitcast.18, f32[]{:T(128)} %constant.68.clone.1), kind=kCustom, calls=%fused_computation.11 | custom fusion | flops 4096 | bytes 196612 | tf_op jit(solution)/shard_map/scatter-add | solution.py:50
  38.8 3.0 %collective-permute-start = (f32[16384]{0:T(1024)S(1)}, f32[16384]{0:T(1024)S(1)}, u32[]{:S(2)}, u32[]{:S(2)}) collective-permute-start(f32[16384]{0:T(1024)S(1)} %get-tuple-element.3), channel_id=1, source_target_pairs={{24,0},{0,8},{8,16},{16,24},{25,1},{1,9},{9,17},{17,25},{26,2},{2,... | collective-permute-start | bytes 196616 | tf_op jit(solution)/shard_map/ppermute | solution.py:14
  41.8 1.0 collective-permute-start.1
  42.8 0.7 dynamic_slice.3
  43.5 1.6 %collective-permute-done = f32[16384]{0:T(1024)S(1)} collective-permute-done((f32[16384]{0:T(1024)S(1)}, f32[16384]{0:T(1024)S(1)}, u32[]{:S(2)}, u32[]{:S(2)}) %collective-permute-start) | collective-permute-done | bytes 65568 | tf_op jit(solution)/shard_map/ppermute | solution.py:14
  45.1 1.4 collective-permute-done.1
  46.5 0.6 fusion.3
  47.2 0.1 select_reduce_fusion
  47.3 0.6 dynamic-slice
  48.5 53.2 %all-reduce.3.cloned.1.call-done = f32[16384]{0:T(1024)} async-done(((f32[16384]{0:T(1024)}), f32[16384]{0:T(1024)}) %all-reduce.3.cloned.1.call-update) | async-done | bytes 65552
  101.7 0.7 fusion.11
  102.4 14.0 %all_gather.3 = f32[16384]{0:T(1024)S(1)} all-gather(f32[2048]{0:T(1024)S(1)} %fusion.11), channel_id=1, replica_groups=mesh['region'=4,'cluster'=8] {'cluster'}, dimensions={0}, use_global_device_ids=true | all-gather | bytes 73728 | tf_op jit(solution)/shard_map/all_gather | solution.py:56
  116.4 1.5 collective-permute-start.2
  117.8 1.5 collective-permute-start.3
  119.3 2.6 %collective-permute-done.2 = f32[16384]{0:T(1024)S(1)} collective-permute-done((f32[16384]{0:T(1024)S(1)}, f32[16384]{0:T(1024)S(1)}, u32[]{:S(2)}, u32[]{:S(2)}) %collective-permute-start.2) | collective-permute-done | bytes 65568 | tf_op jit(solution)/shard_map/ppermute | solution.py:14
  121.9 1.1 collective-permute-done.3
  123.0 23.0 %gather_fusion = f32[4096]{0:T(1024)S(1)} fusion(f32[49152]{0:T(1024)S(1)} %pad_maximum_fusion, s32[4096]{0:T(1024)S(1)} %bitcast_clamp_fusion), kind=kCustom, calls=%fused_computation | custom fusion | bytes 49152 | tf_op jit(solution)/shard_map/gather | solution.py:60
  146.1 0.7 select_convert_fusion
  (23 shorter events, 0.1 us)
Async XLA Ops:
  7.2 7.2 %copy-start.2 = (bf16[4,8,1024]{2,1,0:T(8,128)(2,1)S(1)}, bf16[4,8,1024]{2,1,0:T(8,128)(2,1)}, u32[]{:S(2)}) copy-start(bf16[4,8,1024]{2,1,0:T(8,128)(2,1)} %param.10) | copy-start | bytes 196612
  7.2 94.5 %all-reduce.3.cloned.1.call-start = ((), (), s32[]{:S(2)}) async-start(), calls=%async_computation | async-start | bytes 131072
  7.3 7.1 %copy-start = (bf16[4,1024,1024]{2,1,0:T(8,128)(2,1)S(1)}, bf16[4,1024,1024]{2,1,0:T(8,128)(2,1)}, u32[]{:S(2)}) copy-start(bf16[4,1024,1024]{2,1,0:T(8,128)(2,1)} %param.9) | copy-start | bytes 25165828
  9.1 7.7 %copy-start.4 = (s32[4]{0:T(128)S(1)}, s32[4]{0:T(128)}, u32[]{:S(2)}) copy-start(s32[4]{0:T(128)} %param.12) | copy-start | bytes 52
  9.1 38.1 %copy-start.5 = (f32[16]{0:T(128)S(1)}, f32[16]{0:T(128)}, u32[]{:S(2)}) copy-start(f32[16]{0:T(128)} %param.17) | copy-start | bytes 196
  9.1 38.2 %copy-start.6 = (u32[32]{0:T(128)S(1)}, u32[32]{0:T(128)}, u32[]{:S(2)}) copy-start(u32[32]{0:T(128)} %constant.94) | copy-start | bytes 388
  14.4 131.7 %copy-start.1 = (f32[4,8,1024]{2,1,0:T(8,128)}, f32[4,8,1024]{2,1,0:T(8,128)S(1)}, u32[]{:S(2)}) copy-start(f32[4,8,1024]{2,1,0:T(8,128)S(1)} %get-tuple-element.11) | copy-start | bytes 393220
  38.8 6.3 %collective-permute-start = (f32[16384]{0:T(1024)S(1)}, f32[16384]{0:T(1024)S(1)}, u32[]{:S(2)}, u32[]{:S(2)}) collective-permute-start(f32[16384]{0:T(1024)S(1)} %get-tuple-element.3), channel_id=1, source_target_pairs={{24,0},{0,8},{8,16},{16,24},{25,1},{1,9},{9,17},{17,25},{26,2},{2,... | collective-permute-start | bytes 196616 | tf_op jit(solution)/shard_map/ppermute | solution.py:14
  41.8 4.7 %collective-permute-start.1 = (f32[16384]{0:T(1024)S(1)}, f32[16384]{0:T(1024)S(1)}, u32[]{:S(2)}, u32[]{:S(2)}) collective-permute-start(f32[16384]{0:T(1024)S(1)} %get-tuple-element.4), channel_id=1, source_target_pairs={{8,0},{16,8},{24,16},{0,24},{9,1},{17,9},{25,17},{1,25},{10,2},{18... | collective-permute-start | bytes 196616 | tf_op jit(solution)/shard_map/ppermute | solution.py:14
  102.4 43.7 %copy-start.3 = (f32[2048]{0:T(1024)}, f32[2048]{0:T(1024)S(1)}, u32[]{:S(2)}) copy-start(f32[2048]{0:T(1024)S(1)} %fusion.11) | copy-start | bytes 24580
  116.4 5.5 %collective-permute-start.2 = (f32[16384]{0:T(1024)S(1)}, f32[16384]{0:T(1024)S(1)}, u32[]{:S(2)}, u32[]{:S(2)}) collective-permute-start(f32[16384]{0:T(1024)S(1)} %all_gather.3), channel_id=1, source_target_pairs={{24,0},{0,8},{8,16},{16,24},{25,1},{1,9},{9,17},{17,25},{26,2},{2,... | collective-permute-start | bytes 196616 | tf_op jit(solution)/shard_map/ppermute | solution.py:14
  117.8 5.2 %collective-permute-start.3 = (f32[16384]{0:T(1024)S(1)}, f32[16384]{0:T(1024)S(1)}, u32[]{:S(2)}, u32[]{:S(2)}) collective-permute-start(f32[16384]{0:T(1024)S(1)} %all_gather.3), channel_id=1, source_target_pairs={{8,0},{16,8},{24,16},{0,24},{9,1},{17,9},{25,17},{1,25},{10,2},{18... | collective-permute-start | bytes 196616 | tf_op jit(solution)/shard_map/ppermute | solution.py:14
Sparse Core Ops, SparseCore 0:
  47.3 54.3 all-reduce.2
where the time goes:
time: 154 us
  waiting for transfers between devices  59.9 us (39%)
  other arithmetic  26 us (17%)
  local copies, waits for them, and re-layouts  24.4 us (16%)
  between operations  14.9 us (10%)
  blocking collectives  14 us (9%)
  matrix products  7.59 us (5%)
  starting transfers between devices  6.97 us (5%)
    unnamed x2, waiting for transfers between devices  53.2 us
    gather x2, local copies, waits for them, and re-layouts, local(): rate = nearby[relative]  23 us
    scatter-add x1, other arithmetic, local(): jax.ops.segment_sum(flat_llr, relative.reshape(-1), num_segments=3 * regi...  21.9 us
    all_gather x1, blocking collectives, local(): own_post = lax.all_gather(owned, 'cluster', axis=0, tiled=True)  14 us
    ppermute x4, starting transfers between devices, passed_along(): return lax.ppermute(block, axis, route)  6.94 us
    ppermute x4, waiting for transfers between devices, passed_along(): return lax.ppermute(block, axis, route)  6.68 us
    dot_general x1, matrix products, local(): jnp.einsum('amr,arl->aml', masked, pilots, preferred_element_type=jnp.flo...  5.3 us
  transfers between devices with their start and end apart: 5, of which 5 were waited for; matrix products, arithmetic and copies ran while one was open for 1% of the time, Pallas kernels for 0%

commit v1 on v0

--- a/solution.py
+++ b/solution.py
@@ -1,3 +1,4 @@
+import functools
 import jax
 import jax.numpy as jnp
 from jax import lax
@@ -6,6 +7,23 @@
 ROW_BLOCK = 128
 U_DEV = 2048
 epsilon = 1e-06
+
+
+def register_the_levels_all(row_data, axis_name, dim_at):
+    devs = lax.axis_size(axis_name)
+    seen_now = sorted(((ix, (ix + 1) % devs) for ix in range(devs)))
+    near = row_data
+    items = [near]
+    for d in range(1, devs):
+        near = lax.ppermute(near, axis_name=axis_name, perm=seen_now)
+        items.insert(0, near)
+    x_new = jnp.concatenate(items, axis=dim_at)
+    piece_out = lax.axis_index(axis_name)
+    item_now = piece_out + 1
+    return jnp.roll(x_new, item_now * row_data.shape[dim_at], dim_at)
+
+
+_choose_array = functools.partial(register_the_levels_all, axis_name="cluster", dim_at=0)
 
 
 def passed_along(block, axis, distance):
@@ -53,7 +71,7 @@
     region_sum = window[region_users : 2 * region_users] + from_below + from_above
     owned_sum = lax.psum_scatter(region_sum, "cluster", scatter_dimension=0, tiled=True)
     owned = decide(owned_sum, own_start, U_DEV, user_cluster, cluster_prior)
-    own_post = lax.all_gather(owned, "cluster", axis=0, tiled=True)
+    own_post = _choose_array(owned)
     below = passed_along(own_post, "region", 1)
     above = passed_along(own_post, "region", -1)
     nearby = jnp.concatenate([below, own_post, above])

time: 154 us -> 175 us (1.14)
  waiting for transfers between devices: 59.9 us -> 95.4 us
  blocking collectives: 14 us -> 0 us
    ppermute x0 -> x7, waiting for transfers between devices: none -> 34.1 us  [register_the_levels_all(): near = lax.ppermute(near, axis_name=axis_name, perm=seen_now)]
    all_gather x1 -> x0, blocking collectives: 14 us -> none  [local(): own_post = lax.all_gather(owned, 'cluster', axis=0, tiled=True)]
  transfers between devices with their start and end apart: 5 -> 12, of which waited for: 5 -> 12; matrix products, arithmetic and copies ran while one was open for 1% -> 1% of each run, Pallas kernels for 0% -> 0%
where the time goes in v1:
time: 175 us
  waiting for transfers between devices  95.4 us (55%)
  other arithmetic  26 us (15%)
  local copies, waits for them, and re-layouts  24.4 us (14%)
  between operations  15 us (9%)
  matrix products  7.59 us (4%)
  starting transfers between devices  6.56 us (4%)
    unnamed x2, waiting for transfers between devices  53.2 us
    ppermute x7, waiting for transfers between devices, register_the_levels_all(): near = lax.ppermute(near, axis_name=axis_name, perm=seen_now)  34.1 us
    gather x2, local copies, waits for them, and re-layouts, local(): rate = nearby[relative]  23 us
    scatter-add x1, other arithmetic, local(): jax.ops.segment_sum(flat_llr, relative.reshape(-1), num_segments=3 * regi...  21.9 us
    ppermute x4, waiting for transfers between devices, passed_along(): return lax.ppermute(block, axis, route)  8.14 us
    ppermute x4, starting transfers between devices, passed_along(): return lax.ppermute(block, axis, route)  6.44 us
    dot_general x1, matrix products, local(): jnp.einsum('amr,arl->aml', masked, pilots, preferred_element_type=jnp.flo...  5.3 us
  transfers between devices with their start and end apart: 12, of which 12 were waited for; matrix products, arithmetic and copies ran while one was open for 1% of the time, Pallas kernels for 0%

profile of v1, /device:TPU:0, one launch (start us, length us, event | category | flops | bytes accessed | tf_op | source)
XLA Modules:
  0.0 175.0 jit_solution(8452917627132282199)
XLA Ops:
  7.3 0.9 fusion.7
  8.2 0.9 broadcast_compare_fusion
  9.1 5.3 %multiply_reduce_fusion.1 = (f32[4]{0:T(128)S(1)}, f32[4,8,1024]{2,1,0:T(8,128)S(1)}) fusion(f32[4,8,1024]{2,1,0:T(8,128)} %param.14, f32[4]{0:T(128)} %param.15, f32[4,8,1024]{2,1,0:T(8,128)} %param.13, bf16[4,1024,1024]{2,1,0:T(8,128)(2,1)} %param.9, bf16[4,8,1024]{2,1,0:T(8,128)(2,1)} %param.10, pred[4,1024]{1,0:T(4,128)(4,1)S(1)} %broadcast_compare_fusion), kind=kOutput, calls=%fused_computation.10 | convolution fusion | flops 67305472 | bytes 8851488 | tf_op jit(solution)/shard_map/amr,arl->aml/dot_general | solution.py:52
  14.4 2.3 %multiply_reduce_fusion = (f32[4,1024]{1,0:T(4,128)S(1)}, f32[4,8,1024]{2,1,0:T(8,128)S(1)}) fusion(bf16[4,1024,1024]{2,1,0:T(8,128)(2,1)S(1)} %copy-done, f32[4,8,1024]{2,1,0:T(8,128)S(1)} %get-tuple-element.11, bf16[4,8,1024]{2,1,0:T(8,128)(2,1)S(1)} %copy-done.2, pred[4,1024]{1,0:T(4,128)(4,1)S(1)} %broadcast_compare_fusion), kind=kOutput, calls=%fused_computation.9 | convolution fusion | flops 67301376 | bytes 8736768 | tf_op jit(solution)/shard_map/aml,arl->amr/dot_general | solution.py:56
  16.8 21.9 %scatter_custom_fusion = f32[49152]{0:T(1024)S(1)} fusion(s32[4096]{0:T(1024)S(1)} %bitcast.17, f32[4096]{0:T(1024)S(1)} %bitcast.18, f32[]{:T(128)} %constant.86.clone.1), kind=kCustom, calls=%fused_computation.11 | custom fusion | flops 4096 | bytes 196612 | tf_op jit(solution)/shard_map/scatter-add | solution.py:68
  38.8 3.0 %collective-permute-start = (f32[16384]{0:T(1024)S(1)}, f32[16384]{0:T(1024)S(1)}, u32[]{:S(2)}, u32[]{:S(2)}) collective-permute-start(f32[16384]{0:T(1024)S(1)} %get-tuple-element.3), channel_id=1, source_target_pairs={{24,0},{0,8},{8,16},{16,24},{25,1},{1,9},{9,17},{17,25},{26,2},{2,... | collective-permute-start | bytes 196616 | tf_op jit(solution)/shard_map/ppermute | solution.py:32
  41.8 1.0 collective-permute-start.1
  42.8 0.7 dynamic_slice.7
  43.5 1.6 collective-permute-done
  45.1 1.4 collective-permute-done.1
  48.5 53.2 %all-reduce.3.cloned.1.call-done = f32[16384]{0:T(1024)} async-done(((f32[16384]{0:T(1024)}), f32[16384]{0:T(1024)}) %all-reduce.3.cloned.1.call-update) | async-done | bytes 65552
  101.7 0.7 fusion.11
  102.5 4.9 %collective-permute-done.2 = f32[2048]{0:T(1024)S(1)} collective-permute-done((f32[2048]{0:T(1024)S(1)}, f32[2048]{0:T(1024)S(1)}, u32[]{:S(2)}, u32[]{:S(2)}) %collective-permute-start.2) | collective-permute-done | bytes 8224 | tf_op jit(solution)/shard_map/ppermute | solution.py:18
  107.3 4.9 %collective-permute-done.3 = f32[2048]{0:T(1024)S(1)} collective-permute-done((f32[2048]{0:T(1024)S(1)}, f32[2048]{0:T(1024)S(1)}, u32[]{:S(2)}, u32[]{:S(2)}) %collective-permute-start.3) | collective-permute-done | bytes 8224 | tf_op jit(solution)/shard_map/ppermute | solution.py:18
  112.2 4.9 %collective-permute-done.4 = f32[2048]{0:T(1024)S(1)} collective-permute-done((f32[2048]{0:T(1024)S(1)}, f32[2048]{0:T(1024)S(1)}, u32[]{:S(2)}, u32[]{:S(2)}) %collective-permute-start.4) | collective-permute-done | bytes 8224 | tf_op jit(solution)/shard_map/ppermute | solution.py:18
  117.1 4.9 %collective-permute-done.5 = f32[2048]{0:T(1024)S(1)} collective-permute-done((f32[2048]{0:T(1024)S(1)}, f32[2048]{0:T(1024)S(1)}, u32[]{:S(2)}, u32[]{:S(2)}) %collective-permute-start.5) | collective-permute-done | bytes 8224 | tf_op jit(solution)/shard_map/ppermute | solution.py:18
  121.9 4.9 %collective-permute-done.6 = f32[2048]{0:T(1024)S(1)} collective-permute-done((f32[2048]{0:T(1024)S(1)}, f32[2048]{0:T(1024)S(1)}, u32[]{:S(2)}, u32[]{:S(2)}) %collective-permute-start.6) | collective-permute-done | bytes 8224 | tf_op jit(solution)/shard_map/ppermute | solution.py:18
  126.8 4.9 %collective-permute-done.7 = f32[2048]{0:T(1024)S(1)} collective-permute-done((f32[2048]{0:T(1024)S(1)}, f32[2048]{0:T(1024)S(1)}, u32[]{:S(2)}, u32[]{:S(2)}) %collective-permute-start.7) | collective-permute-done | bytes 8224 | tf_op jit(solution)/shard_map/ppermute | solution.py:18
  131.7 4.9 %collective-permute-done.8 = f32[2048]{0:T(1024)S(1)} collective-permute-done((f32[2048]{0:T(1024)S(1)}, f32[2048]{0:T(1024)S(1)}, u32[]{:S(2)}, u32[]{:S(2)}) %collective-permute-start.8) | collective-permute-done | bytes 8224 | tf_op jit(solution)/shard_map/ppermute | solution.py:18
  136.7 2.4 %collective-permute-start.10 = (f32[16384]{0:T(1024)S(1)}, f32[16384]{0:T(1024)S(1)}, u32[]{:S(2)}, u32[]{:S(2)}) collective-permute-start(f32[16384]{0:T(1024)S(1)} %dynamic_slice.8), channel_id=1, source_target_pairs={{8,0},{16,8},{24,16},{0,24},{9,1},{17,9},{25,17},{1,25},{10,2},{18... | collective-permute-start | bytes 196616 | tf_op jit(solution)/shard_map/ppermute | solution.py:32
  139.2 1.9 %collective-permute-done.10 = f32[16384]{0:T(1024)S(1)} collective-permute-done((f32[16384]{0:T(1024)S(1)}, f32[16384]{0:T(1024)S(1)}, u32[]{:S(2)}, u32[]{:S(2)}) %collective-permute-start.10) | collective-permute-done | bytes 65568 | tf_op jit(solution)/shard_map/ppermute | solution.py:32
  141.1 3.3 %collective-permute-done.9 = f32[16384]{0:T(1024)S(1)} collective-permute-done((f32[16384]{0:T(1024)S(1)}, f32[16384]{0:T(1024)S(1)}, u32[]{:S(2)}, u32[]{:S(2)}) %collective-permute-start.9) | collective-permute-done | bytes 65568 | tf_op jit(solution)/shard_map/ppermute | solution.py:32
  144.3 23.0 %gather_fusion = f32[4096]{0:T(1024)S(1)} fusion(f32[49152]{0:T(1024)S(1)} %pad_maximum_fusion, s32[4096]{0:T(1024)S(1)} %bitcast_clamp_fusion), kind=kCustom, calls=%fused_computation | custom fusion | bytes 49152 | tf_op jit(solution)/shard_map/gather | solution.py:78
  167.4 0.7 select_convert_fusion
  (53 shorter events, 1.7 us)
Async XLA Ops:
  7.2 7.2 %copy-start.2 = (bf16[4,8,1024]{2,1,0:T(8,128)(2,1)S(1)}, bf16[4,8,1024]{2,1,0:T(8,128)(2,1)}, u32[]{:S(2)}) copy-start(bf16[4,8,1024]{2,1,0:T(8,128)(2,1)} %param.10) | copy-start | bytes 196612
  7.2 94.5 %all-reduce.3.cloned.1.call-start = ((), (), s32[]{:S(2)}) async-start(), calls=%async_computation | async-start | bytes 131072
  7.3 7.1 %copy-start = (bf16[4,1024,1024]{2,1,0:T(8,128)(2,1)S(1)}, bf16[4,1024,1024]{2,1,0:T(8,128)(2,1)}, u32[]{:S(2)}) copy-start(bf16[4,1024,1024]{2,1,0:T(8,128)(2,1)} %param.9) | copy-start | bytes 25165828
  9.1 7.7 %copy-start.4 = (s32[4]{0:T(128)S(1)}, s32[4]{0:T(128)}, u32[]{:S(2)}) copy-start(s32[4]{0:T(128)} %param.12) | copy-start | bytes 52
  9.1 38.1 %copy-start.5 = (f32[16]{0:T(128)S(1)}, f32[16]{0:T(128)}, u32[]{:S(2)}) copy-start(f32[16]{0:T(128)} %param.17) | copy-start | bytes 196
  9.1 38.2 %copy-start.6 = (u32[32]{0:T(128)S(1)}, u32[32]{0:T(128)}, u32[]{:S(2)}) copy-start(u32[32]{0:T(128)} %constant.113) | copy-start | bytes 388
  14.4 153.0 %copy-start.1 = (f32[4,8,1024]{2,1,0:T(8,128)}, f32[4,8,1024]{2,1,0:T(8,128)S(1)}, u32[]{:S(2)}) copy-start(f32[4,8,1024]{2,1,0:T(8,128)S(1)} %get-tuple-element.11) | copy-start | bytes 393220
  38.8 6.3 %collective-permute-start = (f32[16384]{0:T(1024)S(1)}, f32[16384]{0:T(1024)S(1)}, u32[]{:S(2)}, u32[]{:S(2)}) collective-permute-start(f32[16384]{0:T(1024)S(1)} %get-tuple-element.3), channel_id=1, source_target_pairs={{24,0},{0,8},{8,16},{16,24},{25,1},{1,9},{9,17},{17,25},{26,2},{2,... | collective-permute-start | bytes 196616 | tf_op jit(solution)/shard_map/ppermute | solution.py:32
  41.8 4.7 %collective-permute-start.1 = (f32[16384]{0:T(1024)S(1)}, f32[16384]{0:T(1024)S(1)}, u32[]{:S(2)}, u32[]{:S(2)}) collective-permute-start(f32[16384]{0:T(1024)S(1)} %get-tuple-element.4), channel_id=1, source_target_pairs={{8,0},{16,8},{24,16},{0,24},{9,1},{17,9},{25,17},{1,25},{10,2},{18... | collective-permute-start | bytes 196616 | tf_op jit(solution)/shard_map/ppermute | solution.py:32
  102.4 65.0 %copy-start.3 = (f32[2048]{0:T(1024)}, f32[2048]{0:T(1024)S(1)}, u32[]{:S(2)}) copy-start(f32[2048]{0:T(1024)S(1)} %fusion.11) | copy-start | bytes 24580
  102.4 4.9 %collective-permute-start.2 = (f32[2048]{0:T(1024)S(1)}, f32[2048]{0:T(1024)S(1)}, u32[]{:S(2)}, u32[]{:S(2)}) collective-permute-start(f32[2048]{0:T(1024)S(1)} %fusion.11), channel_id=1, source_target_pairs={{0,1},{1,2},{2,3},{3,4},{4,5},{5,6},{6,7},{7,0},{8,9},{9,10},{10,1... | collective-permute-start | bytes 24584 | tf_op jit(solution)/shard_map/ppermute | solution.py:18
  107.3 4.9 %collective-permute-start.3 = (f32[2048]{0:T(1024)S(1)}, f32[2048]{0:T(1024)S(1)}, u32[]{:S(2)}, u32[]{:S(2)}) collective-permute-start(f32[2048]{0:T(1024)S(1)} %collective-permute-done.2), channel_id=1, source_target_pairs={{0,1},{1,2},{2,3},{3,4},{4,5},{5,6},{6,7},{7,0},{8,9},{9,10},{10,1... | collective-permute-start | bytes 24584 | tf_op jit(solution)/shard_map/ppermute | solution.py:18
  112.2 4.9 %collective-permute-start.4 = (f32[2048]{0:T(1024)S(1)}, f32[2048]{0:T(1024)S(1)}, u32[]{:S(2)}, u32[]{:S(2)}) collective-permute-start(f32[2048]{0:T(1024)S(1)} %collective-permute-done.3), channel_id=1, source_target_pairs={{0,1},{1,2},{2,3},{3,4},{4,5},{5,6},{6,7},{7,0},{8,9},{9,10},{10,1... | collective-permute-start | bytes 24584 | tf_op jit(solution)/shard_map/ppermute | solution.py:18
  117.1 4.9 %collective-permute-start.5 = (f32[2048]{0:T(1024)S(1)}, f32[2048]{0:T(1024)S(1)}, u32[]{:S(2)}, u32[]{:S(2)}) collective-permute-start(f32[2048]{0:T(1024)S(1)} %collective-permute-done.4), channel_id=1, source_target_pairs={{0,1},{1,2},{2,3},{3,4},{4,5},{5,6},{6,7},{7,0},{8,9},{9,10},{10,1... | collective-permute-start | bytes 24584 | tf_op jit(solution)/shard_map/ppermute | solution.py:18
  121.9 4.9 %collective-permute-start.6 = (f32[2048]{0:T(1024)S(1)}, f32[2048]{0:T(1024)S(1)}, u32[]{:S(2)}, u32[]{:S(2)}) collective-permute-start(f32[2048]{0:T(1024)S(1)} %collective-permute-done.5), channel_id=1, source_target_pairs={{0,1},{1,2},{2,3},{3,4},{4,5},{5,6},{6,7},{7,0},{8,9},{9,10},{10,1... | collective-permute-start | bytes 24584 | tf_op jit(solution)/shard_map/ppermute | solution.py:18
  126.8 4.9 %collective-permute-start.7 = (f32[2048]{0:T(1024)S(1)}, f32[2048]{0:T(1024)S(1)}, u32[]{:S(2)}, u32[]{:S(2)}) collective-permute-start(f32[2048]{0:T(1024)S(1)} %collective-permute-done.6), channel_id=1, source_target_pairs={{0,1},{1,2},{2,3},{3,4},{4,5},{5,6},{6,7},{7,0},{8,9},{9,10},{10,1... | collective-permute-start | bytes 24584 | tf_op jit(solution)/shard_map/ppermute | solution.py:18
  131.7 4.9 %collective-permute-start.8 = (f32[2048]{0:T(1024)S(1)}, f32[2048]{0:T(1024)S(1)}, u32[]{:S(2)}, u32[]{:S(2)}) collective-permute-start(f32[2048]{0:T(1024)S(1)} %collective-permute-done.7), channel_id=1, source_target_pairs={{0,1},{1,2},{2,3},{3,4},{4,5},{5,6},{6,7},{7,0},{8,9},{9,10},{10,1... | collective-permute-start | bytes 24584 | tf_op jit(solution)/shard_map/ppermute | solution.py:18
  136.7 4.3 %collective-permute-start.10 = (f32[16384]{0:T(1024)S(1)}, f32[16384]{0:T(1024)S(1)}, u32[]{:S(2)}, u32[]{:S(2)}) collective-permute-start(f32[16384]{0:T(1024)S(1)} %dynamic_slice.8), channel_id=1, source_target_pairs={{8,0},{16,8},{24,16},{0,24},{9,1},{17,9},{25,17},{1,25},{10,2},{18... | collective-permute-start | bytes 196616 | tf_op jit(solution)/shard_map/ppermute | solution.py:32
  139.2 5.2 %collective-permute-start.9 = (f32[16384]{0:T(1024)S(1)}, f32[16384]{0:T(1024)S(1)}, u32[]{:S(2)}, u32[]{:S(2)}) collective-permute-start(f32[16384]{0:T(1024)S(1)} %dynamic_slice.8), channel_id=1, source_target_pairs={{24,0},{0,8},{8,16},{16,24},{25,1},{1,9},{9,17},{17,25},{26,2},{2,... | collective-permute-start | bytes 196616 | tf_op jit(solution)/shard_map/ppermute | solution.py:32
Sparse Core Ops, SparseCore 0:
  47.3 54.3 all-reduce.2
